TPU v7x, 32 devices: a whole 2x2x4 slice. The times are simulated.
32 devices in a mesh: dp: 4 (over y, x), mp: 8 (over z, core).
Axes of the slice: x: 2, y: 2, z: 4, core: 2. Of those that a mesh axis runs over, the one named last changes fastest.
Arguments:
- inputs: bfloat16 [8, 256, 6144], P('dp', None, 'mp'), may hold values from -6 to 6
- cotangent: bfloat16 [8, 256, 6144], P('dp', None, 'mp'), may hold values from -6 to 6
- w_up: bfloat16 [6144, 24576], P('dp', 'mp'), may hold values from -0.078125 to 0.078125
- w_down: bfloat16 [24576, 6144], P('mp', 'dp'), may hold values from -0.0390625 to 0.0390625
- thresholds: float32 [2], replicated, may hold values from 23592.96 to 58982.4
Outputs:
- grad_up: float32 [6144, 24576], P('dp', 'mp')
- grad_down: float32 [24576, 6144], P('mp', 'dp')
- norms: float32 [8, 2], P('dp')
All inputs are finite; a program needn't handle non-finite values.
Results may differ from a plain program's by a relative error of at most 0.0085.
Values may be sent and summed in bfloat16 or wider, within the bound.
No kernel may reach another device: no remote copies, remote signals or barrier semaphores. Data moves between devices by JAX's collectives and lax.ppermute only.
A program may use at most 256 MiB of HBM per device.

v0:
```python
import jax
import jax.numpy as jnp
from jax import lax
from jax.sharding import PartitionSpec as P

inv_root_two = 0.7071067811865476
inv_root_two_pi = 0.3989422804014327


def normal_cdf(value):
    return 0.5 * (1.0 + lax.erf(value * inv_root_two))


def gram_of(array, images, patches):
    cube = array.reshape(images, patches, -1)
    return jnp.einsum("btd,bsd->bts", cube, cube, preferred_element_type=jnp.float32)


def on_device(inputs, cotangent, w_up, w_down, thresholds):
    images, patches, local_feats = inputs.shape
    count_rows = images * patches
    x_whole = lax.all_gather(inputs, "mp", axis=2, tiled=True).reshape(count_rows, -1)
    hidden_local = w_up.shape[1]
    columns = x_whole
    pre = jnp.dot(
        columns, lax.all_gather(w_up, "dp", axis=0, tiled=True), preferred_element_type=jnp.float32
    )
    act = (pre * normal_cdf(pre)).astype(jnp.bfloat16)
    dy_whole = lax.all_gather(cotangent, "mp", axis=2, tiled=True).reshape(count_rows, -1)
    columns = dy_whole
    dact = lax.dot_general(
        columns,
        lax.all_gather(w_down, "dp", axis=1, tiled=True),
        (((1,), (1,)), ((), ())),
        preferred_element_type=jnp.float32,
    )
    slope = normal_cdf(pre) + pre * jnp.exp(-0.5 * pre * pre) * inv_root_two_pi
    dpre = (dact * slope).astype(jnp.bfloat16)
    gram_dpre = gram_of(dpre, images, patches)
    gram_act = gram_of(act, images, patches)
    part_up = jnp.sum(gram_of(x_whole, images, patches) * gram_dpre, axis=(1, 2))
    part_down = jnp.sum(gram_act * gram_of(dy_whole, images, patches), axis=(1, 2))
    sq_up, sq_down = lax.psum((part_up, part_down), "mp")
    norms = jnp.stack([jnp.sqrt(sq_up), jnp.sqrt(sq_down)], axis=1)
    factor = jnp.minimum(1.0, thresholds[None, :] / (norms + 1e-06))
    dpre_clip = (
        (
            factor[:, 0][:, None, None]
            * dpre.reshape(images, patches, hidden_local).astype(jnp.float32)
        )
        .astype(jnp.bfloat16)
        .reshape(count_rows, hidden_local)
    )
    cot_clip = (
        (factor[:, 1][:, None, None] * dy_whole.reshape(images, patches, -1).astype(jnp.float32))
        .astype(jnp.bfloat16)
        .reshape(count_rows, -1)
    )
    columns = x_whole
    grad_up = lax.psum_scatter(
        lax.dot_general(
            columns, dpre_clip, (((0,), (0,)), ((), ())), preferred_element_type=jnp.float32
        ).astype(jnp.bfloat16),
        "dp",
        scatter_dimension=0,
        tiled=True,
    ).astype(jnp.float32)
    down_full = lax.dot_general(
        act, cot_clip, (((0,), (0,)), ((), ())), preferred_element_type=jnp.float32
    )
    grad_down = lax.psum_scatter(
        down_full.astype(jnp.bfloat16), "dp", scatter_dimension=1, tiled=True
    ).astype(jnp.float32)
    return (grad_up, grad_down, norms)


def solution(mesh):
    in_specs = (P("dp", None, "mp"), P("dp", None, "mp"), P("dp", "mp"), P("mp", "dp"), P())
    out_specs = (P("dp", "mp"), P("mp", "dp"), P("dp", None))
    return jax.shard_map(
        on_device, mesh=mesh, in_specs=in_specs, out_specs=out_specs, check_vma=False
    )
```

profile of v0, /device:TPU:0, one launch (start us, length us, event | category | flops | bytes accessed | tf_op | source)
XLA Modules:
  0.0 1558.8 jit_solution(477519398786530075)
XLA Ops:
  7.2 0.7 all-gather.5.cloned.1.call-update
  7.9 0.0 all-gather.11.cloned.1.call-start
  7.9 0.7 all-gather.11.cloned.1.call-update
  8.6 0.0 all-gather.7.cloned.1.call-start
  8.7 0.7 all-gather.7.cloned.1.call-update
  9.4 0.0 all-gather.9.cloned.1.call-start
  9.4 0.5 all-gather.9.cloned.1.call-update
  10.0 0.0 reduce-scatter.3.cloned.1.call-start
  10.0 67.0 %all-gather.5.cloned.1.call-done = bf16[2,256,6144]{2,1,0:T(8,128)(2,1)} async-done(((bf16[2,256,768]{2,1,0:T(8,128)(2,1)}), bf16[2,256,6144]{2,1,0:T(8,128)(2,1)}) %all-gather.5.cloned.1.call-update) | async-done | bytes 6291472 | tf_op jit(solution)/shard_map/all_gather | solution.py:22
  77.0 7.2 fusion.10
  84.3 326.2 %all-gather.11.cloned.1.call-done = bf16[6144,3072]{1,0:T(8,128)(2,1)} async-done(((bf16[1536,3072]{1,0:T(8,128)(2,1)}), bf16[6144,3072]{1,0:T(8,128)(2,1)}) %all-gather.11.cloned.1.call-update) | async-done | bytes 37748752 | tf_op jit(solution)/shard_map/all_gather | solution.py:26
  410.4 27.0 %multiply_convert_fusion.2 = (bf16[512,3072]{1,0:T(8,128)(2,1)S(1)}, f32[512,3072]{1,0:T(8,128)}) fusion(bf16[512,6144]{1,0:T(8,128)(2,1)} %bitcast.39, bf16[6144,3072]{1,0:T(8,128)(2,1)} %all-gather.11.cloned.1.call-done), kind=kOutput, calls=%fused_computation.12 | convolution fusion | flops 19335217152 | bytes 53477376 | tf_op jit(solution)/shard_map/dot_general | solution.py:25
  437.4 1.8 fusion.11
  439.2 37.5 %all-gather.7.cloned.1.call-done = bf16[2,256,6144]{2,1,0:T(8,128)(2,1)} async-done(((bf16[2,256,768]{2,1,0:T(8,128)(2,1)}), bf16[2,256,6144]{2,1,0:T(8,128)(2,1)}) %all-gather.7.cloned.1.call-update) | async-done | bytes 6291472 | tf_op jit(solution)/shard_map/all_gather | solution.py:29
  476.8 333.2 %all-gather.9.cloned.1.call-done = bf16[3072,6144]{1,0:T(8,128)(2,1)} async-done(((bf16[3072,1536]{1,0:T(8,128)(2,1)}), bf16[3072,6144]{1,0:T(8,128)(2,1)}) %all-gather.9.cloned.1.call-update) | async-done | bytes 37748752 | tf_op jit(solution)/shard_map/all_gather | solution.py:33
  810.0 28.4 %fusion.6 = bf16[512,3072]{1,0:T(8,128)(2,1)} fusion(f32[512,3072]{1,0:T(8,128)} %get-tuple-element.13, bf16[512,6144]{1,0:T(8,128)(2,1)} %bitcast.35, bf16[3072,6144]{1,0:T(8,128)(2,1)} %all-gather.9.cloned.1.call-done), kind=kOutput, calls=%fused_computation.10 | convolution fusion | flops 19343081472 | bytes 53477376 | tf_op jit(solution)/shard_map/dot_general | solution.py:31
  838.4 4.1 fusion.8
  842.5 0.5 copy-done
  843.1 0.1 copy-done.1
  843.1 1.9 fusion.9
  845.1 4.8 copy.8
  849.9 16.2 %all-reduce = (f32[2]{0:T(128)S(1)}, f32[2]{0:T(128)S(1)}) all-reduce(f32[2]{0:T(128)S(1)} %fusion.9, f32[2]{0:T(128)S(1)} %fusion.8), channel_id=1, replica_groups=mesh['dp'=4,'mp'=8] {'mp'}, use_global_device_ids=true, to_apply=%region_3.0 | all-reduce | flops 4 | bytes 32 | tf_op jit(solution)/shard_map/psum | solution.py:43
  866.1 0.1 pad_maximum_fusion
  866.1 27.4 %fusion = bf16[6144,3072]{0,1:T(8,128)(2,1)} fusion(bf16[2,256,6144]{2,1,0:T(8,128)(2,1)} %all-gather.5.cloned.1.call-done, bf16[2,256,3072]{1,2,0:T(8,128)(2,1)} %copy.8, f32[2]{0:T(128)S(1)} %get-tuple-element.11), kind=kOutput, calls=%fused_computation.2 | convolution fusion | flops 19350945792 | bytes 47185928 | tf_op jit(solution)/shard_map/dot_general | solution.py:61
  893.6 0.0 reduce-scatter.5.cloned.1.call-start
  893.6 7.2 multiply_convert_fusion
  900.8 26.9 %convolution_convert_fusion = bf16[3072,6144]{1,0:T(8,128)(2,1)} fusion(bf16[512,3072]{1,0:T(8,128)(2,1)S(1)} %get-tuple-element.12, bf16[512,6144]{1,0:T(8,128)(2,1)} %bitcast.36), kind=kOutput, calls=%fused_computation.1 | convolution fusion | flops 19346227200 | bytes 47185920 | tf_op jit(solution)/shard_map/dot_general | solution.py:68
  927.7 0.6 copy.10
  928.4 285.0 %reduce-scatter.3.cloned.1.call-done = bf16[1536,3072]{0,1:T(8,128)(2,1)} async-done(((bf16[6144,3072]{0,1:T(8,128)(2,1)}), bf16[1536,3072]{0,1:T(8,128)(2,1)}) %reduce-scatter.3.cloned.1.call-update) | async-done | bytes 9437200 | tf_op jit(solution)/shard_map/reduce_scatter | solution.py:60
  1213.4 13.8 copy.9
  1227.2 311.6 %reduce-scatter.5.cloned.1.call-done = bf16[3072,1536]{1,0:T(8,128)(2,1)} async-done(((bf16[3072,6144]{1,0:T(8,128)(2,1)}), bf16[3072,1536]{1,0:T(8,128)(2,1)}) %reduce-scatter.5.cloned.1.call-update) | async-done | bytes 9437200 | tf_op jit(solution)/shard_map/reduce_scatter | solution.py:71
  1538.8 13.2 convert_element_type.43
  (11 shorter events, 0.1 us)
Async XLA Ops:
  7.2 69.9 %all-gather.5.cloned.1.call-start = ((), (), s32[]{:S(2)}) async-start(), calls=%async_computation.2 | async-start | bytes 7077888 | tf_op jit(solution)/shard_map/all_gather | solution.py:22
  7.9 402.5 %all-gather.11.cloned.1.call-start = ((), (), s32[]{:S(2)}) async-start(), calls=%async_computation.5 | async-start | bytes 47185920 | tf_op jit(solution)/shard_map/all_gather | solution.py:26
  8.6 468.1 %all-gather.7.cloned.1.call-start = ((), (), s32[]{:S(2)}) async-start(), calls=%async_computation.3 | async-start | bytes 7077888 | tf_op jit(solution)/shard_map/all_gather | solution.py:29
  9.4 800.6 %all-gather.9.cloned.1.call-start = ((), (), s32[]{:S(2)}) async-start(), calls=%async_computation.4 | async-start | bytes 47185920 | tf_op jit(solution)/shard_map/all_gather | solution.py:33
  10.0 1203.4 %reduce-scatter.3.cloned.1.call-start = ((), (), s32[]{:S(2)}) async-start(), calls=%async_computation.6 | async-start | bytes 47185920 | tf_op jit(solution)/shard_map/reduce_scatter | solution.py:60
  810.0 28.4 %copy-start.3 = (f32[2,256,256]{2,1,0:T(8,128)S(1)}, f32[2,256,256]{2,1,0:T(8,128)}, u32[]{:S(2)}) copy-start(f32[2,256,256]{2,1,0:T(8,128)} %fusion.10) | copy-start | bytes 1572868
  838.4 4.6 copy-start
  838.4 4.7 copy-start.1
  845.1 21.0 %copy-start.2 = (f32[2]{0:T(128)S(1)}, f32[2]{0:T(128)}, u32[]{:S(2)}) copy-start(f32[2]{0:T(128)} %param.9) | copy-start | bytes 28
  893.6 645.2 %reduce-scatter.5.cloned.1.call-start = ((), (), s32[]{:S(2)}) async-start(), calls=%async_computation.7 | async-start | bytes 47185920 | tf_op jit(solution)/shard_map/reduce_scatter | solution.py:71
Sparse Core Ops, SparseCore 0:
  9.6 67.4 all-gather.4
  78.9 331.4 all-gather.10
  412.1 64.6 all-gather.6
  478.5 331.4 all-gather.8
  893.7 319.6 reduce-scatter.2
  1216.3 322.3 reduce-scatter.4
where the time goes:
time: 1560 us
  waiting for transfers between devices  1360 us (87%)
  matrix products  125 us (8%)
  other arithmetic  20.5 us (1%)
  local copies, waits for them, and re-layouts  19.9 us (1%)
  blocking collectives  16.2 us (1%)
    all_gather x1, waiting for transfers between devices, on_device(): lax.all_gather(w_down, 'dp', axis=1, tiled=True)  333 us
    all_gather x1, waiting for transfers between devices, on_device(): lax.all_gather(w_up, 'dp', axis=0, tiled=True)  326 us
    reduce_scatter x1, waiting for transfers between devices, on_device(): lax.psum_scatter(down_full.astype(jnp.bfloat16), 'dp', scatter_dimension=...  312 us
    reduce_scatter x1, waiting for transfers between devices, on_device(): lax.psum_scatter(lax.dot_general(columns, dpre_clip, (((0,), (0,)), ((),...  285 us
    all_gather x1, waiting for transfers between devices, on_device(): lax.all_gather(inputs, 'mp', axis=2, tiled=True).reshape(count_rows, -1)  67 us
    all_gather x1, waiting for transfers between devices, on_device(): lax.all_gather(cotangent, 'mp', axis=2, tiled=True).reshape(count_rows, -1)  37.5 us
  transfers between devices with their start and end apart: 6, of which 6 were waited for; matrix products, arithmetic and copies ran while one was open for 5% of the time, Pallas kernels for 0%

commit v1 on v0

v1 whole, which is shorter than its diff:
```python
import jax
import jax.numpy as jnp
from jax import lax
from jax.sharding import PartitionSpec as P


inv_root_two = 0.7071067811865476
inv_root_two_pi = 0.3989422804014327
f32 = jnp.float32
bf16 = jnp.bfloat16


def normal_cdf(value):
    return 0.5 * (1.0 + lax.erf(value * inv_root_two))


def shift_dp(value, flip):
    count = lax.axis_size("dp")
    return lax.ppermute(value, "dp", [(g, g ^ flip) for g in range(count)])


def swap_mp(value, flip):
    count = lax.axis_size("mp")
    return lax.ppermute(value, "mp", [(m, m ^ flip) for m in range(count)])


def sum_mp(value):
    flip = 1
    while flip < lax.axis_size("mp"):
        value = value + swap_mp(value, flip)
        flip *= 2
    return value


def rows_dot(left, right):
    return jnp.dot(left, right, preferred_element_type=f32)


def rows_dot_t(left, right):
    return lax.dot_general(left, right, (((1,), (1,)), ((), ())), preferred_element_type=f32)


def outer_dot(left, right):
    return lax.dot_general(left, right, (((0,), (0,)), ((), ())), preferred_element_type=f32)


def gram(value):
    return rows_dot_t(value, value)


def pick(stack, index):
    return lax.dynamic_index_in_dim(stack, index, 0, keepdims=False)


def spread(block, groups):
    me, count_mp = lax.axis_index("dp"), lax.axis_size("mp")
    if count_mp == 2 * groups:
        core, line = lax.axis_index("mp") % 2, lax.axis_index("mp") // 2

        def at(g, z, c):
            return g * count_mp + 2 * z + c

        found = []
        for flip in range(groups):
            pairs = [
                (at(g, z, c), at(z, g ^ flip, c))
                for g in range(groups)
                for z in range(groups)
                for c in range(2)
            ]
            found.append(lax.ppermute(block, ("dp", "mp"), pairs))
        mine = jnp.stack(found)
        other = swap_mp(mine, 1)
        first = core == 0
        parts = []
        for r in range(groups):
            index = r ^ (line ^ me)
            one, two = pick(mine, index), pick(other, index)
            parts.append(jnp.concatenate([jnp.where(first, one, two), jnp.where(first, two, one)], axis=1))
        return lax.optimization_barrier(parts)
    whole = lax.all_gather(block, "mp", axis=1, tiled=True)
    stack = whole.reshape(whole.shape[0], groups, -1).transpose(1, 0, 2)
    parts = [pick(stack, me ^ flip) for flip in range(groups)]
    return [parts[0]] + [shift_dp(parts[flip], flip) for flip in range(1, groups)]


def reduce_rows(partials, near, far):
    last = near ^ far
    from_near_far = shift_dp(partials[last].astype(bf16), near)
    from_near = shift_dp(partials[near].astype(bf16), near)
    from_far = shift_dp((partials[far] + from_near_far.astype(f32)).astype(bf16), far)
    return partials[0] + from_near.astype(f32) + from_far.astype(f32)


def gather_rows(own, near, far):
    from_near = shift_dp(own, near)
    from_far = shift_dp(own, far)
    from_both = shift_dp(from_near, far)
    found = {0: own, near: from_near, far: from_far, near ^ far: from_both}
    return [found[r] for r in range(4)]


def on_device(inputs, cotangent, w_up, w_down, thresholds):
    groups = lax.axis_size("dp")
    images, patches, feats = inputs.shape
    routes = [(1, 2) if a % 2 == 0 else (2, 1) for a in range(images)]
    image = [slice(a * patches, (a + 1) * patches) for a in range(images)]

    order = (3, 1, 2, 0)

    x_rows, pre = [], []
    for a in range(images):
        x_rows.append(spread(inputs[a], groups))
        partial = {r: rows_dot(x_rows[a][r], w_up) for r in order}
        pre.append(reduce_rows(partial, *routes[a]))

    y_rows = spread(cotangent.reshape(images * patches, feats), groups)
    partial = {r: rows_dot_t(y_rows[r], w_down) for r in order}
    dact = [
        reduce_rows([partial[r][image[a]] for r in range(groups)], *routes[a])
        for a in range(images)
    ]
    own = [inputs[a] for a in range(images)] + [cotangent[a] for a in range(images)]
    grams = sum_mp(jnp.stack([gram(rows) for rows in own]))

    def clip(rows, grams_of, which):
        part = jnp.stack([jnp.sum(grams_of[a] * gram(rows[a])) for a in range(images)])
        norms = jnp.sqrt(sum_mp(part))
        factor = jnp.minimum(1.0, thresholds[which] / (norms + 1e-06))
        return [(factor[a] * rows[a].astype(f32)).astype(bf16) for a in range(images)], norms

    act = [(p * normal_cdf(p)).astype(bf16) for p in pre]
    act_clip, norms_down = clip(act, grams[images:], 1)
    act_rows = [gather_rows(act_clip[a], *routes[a]) for a in range(images)]
    dpre = [
        (d * (normal_cdf(p) + p * jnp.exp(-0.5 * p * p) * inv_root_two_pi)).astype(bf16)
        for p, d in zip(pre, dact)
    ]
    dpre_clip, norms_up = clip(dpre, grams[:images], 0)
    dpre_rows = [gather_rows(dpre_clip[a], *routes[a]) for a in range(images)]

    def flat(wanted):
        return jnp.concatenate(wanted, axis=0)

    def hidden(rows, wanted):
        return flat([rows[a][r] for r in wanted for a in range(images)])

    every, early, late = list(range(groups)), list(range(groups - 1)), [groups - 1]
    grad_down = outer_dot(hidden(act_rows, every), flat(y_rows))
    grad_up = outer_dot(hidden(x_rows, early), hidden(dpre_rows, early))
    grad_up = grad_up + outer_dot(hidden(x_rows, late), hidden(dpre_rows, late))
    return (grad_up, grad_down, jnp.stack([norms_up, norms_down], axis=1))


def solution(mesh):
    assert mesh.shape["dp"] == 4
    in_specs = (P("dp", None, "mp"), P("dp", None, "mp"), P("dp", "mp"), P("mp", "dp"), P())
    out_specs = (P("dp", "mp"), P("mp", "dp"), P("dp", None))

    return jax.shard_map(on_device, mesh=mesh, in_specs=in_specs, out_specs=out_specs, check_vma=False)
```

time: 1560 us -> 725 us (0.46)
  waiting for transfers between devices: 1360 us -> 311 us
  starting transfers between devices: 0.23 us -> 204 us
  other arithmetic: 20.5 us -> 43.6 us
  blocking collectives: 16.2 us -> 0 us
    all_gather x4 -> x0, waiting for transfers between devices: 764 us -> none  [the longest x1 333 us: on_device(): lax.all_gather(w_down, 'dp', axis=1, tiled=True)]
    reduce_scatter x2 -> x0, waiting for transfers between devices: 597 us -> none  [the longest x1 312 us: on_device(): lax.psum_scatter(down_full.astype(jnp.bfloat16), 'dp', scatter_dimension=...]
    ppermute x0 -> x48, waiting for transfers between devices: none -> 311 us  [the longest x24 275 us: shift_dp(): return lax.ppermute(value, 'dp', [(g, g ^ flip) for g in range(count)])]
    ppermute x0 -> x48, starting transfers between devices: none -> 204 us  [the longest x12 140 us: spread(): found.append(lax.ppermute(block, ('dp', 'mp'), pairs))]
    psum x1 -> x0, blocking collectives: 16.2 us -> none  [on_device(): sq_up, sq_down = lax.psum((part_up, part_down), 'mp')]
    dot_general x8 -> x23, matrix products: 125 us -> 132 us  [the longest x3 59.8 us: outer_dot(): lax.dot_general(left, right, (((0,), (0,)), ((), ())), preferred_element_...]
  transfers between devices with their start and end apart: 6 -> 48, of which waited for: 6 -> 17; matrix products, arithmetic and copies ran while one was open for 5% -> 25% of each run, Pallas kernels for 0% -> 0%
where the time goes in v1:
time: 725 us; the launch traced here: 722 us
  waiting for transfers between devices  311 us (43%)
  starting transfers between devices  204 us (28%)
  matrix products  132 us (18%)
  other arithmetic  43.6 us (6%)
  local copies, waits for them, and re-layouts  29.9 us (4%)
    ppermute x24, waiting for transfers between devices, shift_dp(): return lax.ppermute(value, 'dp', [(g, g ^ flip) for g in range(count)])  275 us
    ppermute x12, starting transfers between devices, spread(): found.append(lax.ppermute(block, ('dp', 'mp'), pairs))  140 us
    dot_general x3, matrix products, outer_dot(): lax.dot_general(left, right, (((0,), (0,)), ((), ())), preferred_element_...  59.8 us
    dot_general x12, matrix products, rows_dot_t(): lax.dot_general(left, right, (((1,), (1,)), ((), ())), preferred_element_...  40.5 us
    ppermute x12, starting transfers between devices, swap_mp(): return lax.ppermute(value, 'mp', [(m, m ^ flip) for m in range(count)])  39.1 us
    ppermute x12, waiting for transfers between devices, spread(): found.append(lax.ppermute(block, ('dp', 'mp'), pairs))  32.2 us
    dot_general x8, matrix products, rows_dot(): return jnp.dot(left, right, preferred_element_type=f32)  31.2 us
    ppermute x24, starting transfers between devices, shift_dp(): return lax.ppermute(value, 'dp', [(g, g ^ flip) for g in range(count)])  25 us
  transfers between devices with their start and end apart: 48, of which 17 were waited for; matrix products, arithmetic and copies ran while one was open for 25% of the time, Pallas kernels for 0%

profile of v1, /device:TPU:0, one launch (start us, length us, event | category | flops | bytes accessed | tf_op | source)
XLA Modules:
  0.0 722.1 jit_solution(11656961535294218439)
XLA Ops:
  2.5 5.7 collective-permute-start.1
  17.7 17.9 %collective-permute-start.14 = (bf16[512,768]{1,0:T(8,128)(2,1)}, bf16[512,768]{1,0:T(8,128)(2,1)}, u32[]{:S(2)}, u32[]{:S(2)}) collective-permute-start(bf16[512,768]{1,0:T(8,128)(2,1)} %bitcast.34), channel_id=1, source_target_pairs={{0,2},{1,3},{2,10},{3,11},{4,18},{5,19},{6,26},{7,27},{8,0},{9,1},... | collective-permute-start | bytes 2359304 | tf_op jit(solution)/shard_map/ppermute | solution.py:71
  35.7 8.9 %collective-permute-start.6 = (bf16[256,768]{1,0:T(8,128)(2,1)S(1)}, bf16[256,768]{1,0:T(8,128)(2,1)S(1)}, u32[]{:S(2)}, u32[]{:S(2)}) collective-permute-start(bf16[256,768]{1,0:T(8,128)(2,1)S(1)} %get-tuple-element.72), channel_id=1, source_target_pairs={{0,2},{1,3},{2,10},{3,11},{4,18},{5,19},{6,26},{7,27},{8,0},{9,1},... | collective-permute-start | bytes 1179656 | tf_op jit(solution)/shard_map/ppermute | solution.py:71
  44.5 57.4 %collective-permute-start.7 = (bf16[256,768]{1,0:T(8,128)(2,1)S(1)}, bf16[256,768]{1,0:T(8,128)(2,1)S(1)}, u32[]{:S(2)}, u32[]{:S(2)}) collective-permute-start(bf16[256,768]{1,0:T(8,128)(2,1)S(1)} %get-tuple-element.72), channel_id=1, source_target_pairs={{0,4},{1,5},{2,12},{3,13},{4,20},{5,21},{6,28},{7,29},{8,6},{9,7},... | collective-permute-start | bytes 1179656 | tf_op jit(solution)/shard_map/ppermute | solution.py:71
  105.2 40.9 %collective-permute-start.15 = (bf16[512,768]{1,0:T(8,128)(2,1)}, bf16[512,768]{1,0:T(8,128)(2,1)}, u32[]{:S(2)}, u32[]{:S(2)}) collective-permute-start(bf16[512,768]{1,0:T(8,128)(2,1)} %bitcast.34), channel_id=1, source_target_pairs={{0,4},{1,5},{2,12},{3,13},{4,20},{5,21},{6,28},{7,29},{8,6},{9,7},... | collective-permute-start | bytes 2359304 | tf_op jit(solution)/shard_map/ppermute | solution.py:71
  149.5 32.0 %collective-permute-done.15 = bf16[512,768]{1,0:T(8,128)(2,1)} collective-permute-done((bf16[512,768]{1,0:T(8,128)(2,1)}, bf16[512,768]{1,0:T(8,128)(2,1)}, u32[]{:S(2)}, u32[]{:S(2)}) %collective-permute-start.15) | collective-permute-done | bytes 786464 | tf_op jit(solution)/shard_map/ppermute | solution.py:71
  185.2 32.9 %collective-permute-start.11 = (f32[4,256,256]{2,1,0:T(8,128)S(1)}, f32[4,256,256]{2,1,0:T(8,128)S(1)}, u32[]{:S(2)}, u32[]{:S(2)}) collective-permute-start(f32[4,256,256]{2,1,0:T(8,128)S(1)} %fusion.46), channel_id=1, source_target_pairs={{0,2},{1,3},{2,0},{3,1},{4,6},{5,7},{6,4},{7,5},{8,10},{9,11},{10,... | collective-permute-start | bytes 3145736 | tf_op jit(solution)/shard_map/ppermute | solution.py:24
  232.0 3.9 convolution_convert_fusion.3
  235.9 3.7 convolution_convert_fusion.2
  239.7 4.4 fusion.56
  244.2 3.9 convolution_convert_fusion.4
  251.7 15.9 %collective-permute-done.28 = bf16[256,3072]{1,0:T(8,128)(2,1)} collective-permute-done((bf16[256,3072]{1,0:T(8,128)(2,1)}, bf16[256,3072]{1,0:T(8,128)(2,1)}, u32[]{:S(2)}, u32[]{:S(2)}) %collective-permute-start.28) | collective-permute-done | bytes 1572896 | tf_op jit(solution)/shard_map/ppermute | solution.py:19
  267.6 4.9 add_convert_fusion
  273.4 3.9 add_convert_fusion.1
  279.7 9.6 %convolution_convert_fusion = bf16[512,3072]{1,0:T(8,128)(2,1)S(1)} fusion(bf16[512,1536]{1,0:T(8,128)(2,1)S(1)} %get-tuple-element.24, bf16[3072,1536]{1,0:T(8,128)(2,1)} %param.8), kind=kOutput, calls=%fused_computation.11 | convolution fusion | flops 4833411072 | bytes 14155776 | tf_op jit(solution)/shard_map/dot_general | solution.py:40
  294.8 7.7 %fusion.52 = f32[512,3072]{1,0:T(8,128)S(1)} fusion(bf16[512,1536]{1,0:T(8,128)(2,1)S(1)} %get-tuple-element.22, bf16[3072,1536]{1,0:T(8,128)(2,1)} %param.8), kind=kOutput, calls=%fused_computation.155 | convolution fusion | flops 4831838208 | bytes 17301504 | tf_op jit(solution)/shard_map/dot_general | solution.py:40
  302.7 7.7 %fusion.53 = f32[512,3072]{1,0:T(8,128)S(1)} fusion(bf16[512,1536]{1,0:T(8,128)(2,1)S(1)} %get-tuple-element.23, bf16[3072,1536]{1,0:T(8,128)(2,1)} %param.8), kind=kOutput, calls=%fused_computation.156 | convolution fusion | flops 4831838208 | bytes 17301504 | tf_op jit(solution)/shard_map/dot_general | solution.py:40
  310.6 29.6 %collective-permute-done.19 = bf16[256,3072]{1,0:T(8,128)(2,1)} collective-permute-done((bf16[256,3072]{1,0:T(8,128)(2,1)}, bf16[256,3072]{1,0:T(8,128)(2,1)}, u32[]{:S(2)}, u32[]{:S(2)}) %collective-permute-start.19) | collective-permute-done | bytes 1572896 | tf_op jit(solution)/shard_map/ppermute | solution.py:19
  349.5 27.9 %collective-permute-done.29 = bf16[256,3072]{1,0:T(8,128)(2,1)S(1)} collective-permute-done((bf16[256,3072]{1,0:T(8,128)(2,1)S(1)}, bf16[256,3072]{1,0:T(8,128)(2,1)S(1)}, u32[]{:S(2)}, u32[]{:S(2)}) %collective-permute-start.29) | collective-permute-done | bytes 1572896 | tf_op jit(solution)/shard_map/ppermute | solution.py:19
  379.9 7.8 %fusion.51 = f32[512,3072]{1,0:T(8,128)S(1)} fusion(bf16[512,1536]{1,0:T(8,128)(2,1)S(1)} %copy-done.13, bf16[3072,1536]{1,0:T(8,128)(2,1)} %param.8), kind=kOutput, calls=%fused_computation.154 | convolution fusion | flops 4831838208 | bytes 17301504 | tf_op jit(solution)/shard_map/dot_general | solution.py:40
  387.8 23.5 %collective-permute-done.18 = bf16[256,3072]{1,0:T(8,128)(2,1)} collective-permute-done((bf16[256,3072]{1,0:T(8,128)(2,1)S(1)}, bf16[256,3072]{1,0:T(8,128)(2,1)}, u32[]{:S(2)}, u32[]{:S(2)}) %collective-permute-start.18) | collective-permute-done | bytes 1572896 | tf_op jit(solution)/shard_map/ppermute | solution.py:19
  414.8 32.1 %collective-permute-done.20 = bf16[256,3072]{1,0:T(8,128)(2,1)} collective-permute-done((bf16[256,3072]{1,0:T(8,128)(2,1)}, bf16[256,3072]{1,0:T(8,128)(2,1)}, u32[]{:S(2)}, u32[]{:S(2)}) %collective-permute-start.20) | collective-permute-done | bytes 1572896 | tf_op jit(solution)/shard_map/ppermute | solution.py:19
  446.9 7.0 fusion.19
  492.8 23.2 %collective-permute-done.33 = bf16[256,3072]{1,0:T(8,128)(2,1)} collective-permute-done((bf16[256,3072]{1,0:T(8,128)(2,1)}, bf16[256,3072]{1,0:T(8,128)(2,1)}, u32[]{:S(2)}, u32[]{:S(2)}) %collective-permute-start.33) | collective-permute-done | bytes 1572896 | tf_op jit(solution)/shard_map/ppermute | solution.py:19
  520.3 29.4 %collective-permute-done.34 = bf16[256,3072]{1,0:T(8,128)(2,1)} collective-permute-done((bf16[256,3072]{1,0:T(8,128)(2,1)}, bf16[256,3072]{1,0:T(8,128)(2,1)}, u32[]{:S(2)}, u32[]{:S(2)}) %collective-permute-start.34) | collective-permute-done | bytes 1572896 | tf_op jit(solution)/shard_map/ppermute | solution.py:19
  553.3 30.2 %collective-permute-done.42 = bf16[256,3072]{1,0:T(8,128)(2,1)} collective-permute-done((bf16[256,3072]{1,0:T(8,128)(2,1)}, bf16[256,3072]{1,0:T(8,128)(2,1)}, u32[]{:S(2)}, u32[]{:S(2)}) %collective-permute-start.42) | collective-permute-done | bytes 1572896 | tf_op jit(solution)/shard_map/ppermute | solution.py:19
  590.7 20.6 %fusion.58 = f32[1536,3072]{1,0:T(8,128)} fusion(bf16[1536,1536]{1,0:T(8,128)(2,1)S(1)} %bitcast.164, bf16[1536,3072]{1,0:T(8,128)(2,1)} %constant_dynamic-update-slice_fusion.6), kind=kOutput, calls=%fused_computation.161 | convolution fusion | flops 14495514624 | bytes 33030144 | tf_op jit(solution)/shard_map/dot_general | solution.py:44
  612.2 8.4 %collective-permute-done.45 = bf16[256,3072]{1,0:T(8,128)(2,1)S(1)} collective-permute-done((bf16[256,3072]{1,0:T(8,128)(2,1)S(1)}, bf16[256,3072]{1,0:T(8,128)(2,1)S(1)}, u32[]{:S(2)}, u32[]{:S(2)}) %collective-permute-start.45) | collective-permute-done | bytes 1572896 | tf_op jit(solution)/shard_map/ppermute | solution.py:19
  629.3 25.1 %collective-permute-done.46 = bf16[256,3072]{1,0:T(8,128)(2,1)S(1)} collective-permute-done((bf16[256,3072]{1,0:T(8,128)(2,1)}, bf16[256,3072]{1,0:T(8,128)(2,1)S(1)}, u32[]{:S(2)}, u32[]{:S(2)}) %collective-permute-start.46) | collective-permute-done | bytes 1572896 | tf_op jit(solution)/shard_map/ppermute | solution.py:19
  655.6 25.6 %collective-permute-done.47 = bf16[256,3072]{1,0:T(8,128)(2,1)S(1)} collective-permute-done((bf16[256,3072]{1,0:T(8,128)(2,1)S(1)}, bf16[256,3072]{1,0:T(8,128)(2,1)S(1)}, u32[]{:S(2)}, u32[]{:S(2)}) %collective-permute-start.47) | collective-permute-done | bytes 1572896 | tf_op jit(solution)/shard_map/ppermute | solution.py:19
  682.6 26.0 %fusion = f32[3072,1536]{1,0:T(8,128)} fusion(bf16[2048,3072]{1,0:T(8,128)(2,1)} %constant_dynamic-update-slice_fusion.12, bf16[512,1536]{1,0:T(8,128)(2,1)S(1)} %copy-done.12, bf16[512,1536]{1,0:T(8,128)(2,1)S(1)} %copy-done.10, bf16[512,1536]{1,0:T(8,128)(2,1)S(1)} %copy-done.16, bf16[512,1536]{1,0:T(8,128)(2,1)S(1)} %copy-done.14), kind=kOutput, calls=%fused_computation.1 | convolution fusion | flops 19352518656 | bytes 37748736 | tf_op jit(solution)/shard_map/dot_general | solution.py:44
  708.6 13.2 %convolution_add_fusion = f32[1536,3072]{1,0:T(8,128)} fusion(f32[1536,3072]{1,0:T(8,128)} %fusion.58, bf16[256,3072]{1,0:T(8,128)(2,1)S(1)} %collective-permute-done.38, bf16[256,3072]{1,0:T(8,128)(2,1)S(1)} %collective-permute-done.37, bf16[256,1536]{1,0:T(8,128)(2,1)S(1)} %copy-done.1, bf16[256,1536]{1,0:T(8,128)(2,1)S(1)} %pad_maximum_fusion.11), kind=kOutput, calls=%fused_computation | convolution fusion | flops 4845993984 | bytes 42467328 | tf_op jit(solution)/shard_map/dot_general | solution.py:44
  (206 shorter events, 129.5 us)
Async XLA Ops:
  13.6 88.3 %collective-permute-start.5 = (bf16[256,768]{1,0:T(8,128)(2,1)S(1)}, bf16[256,768]{1,0:T(8,128)(2,1)S(1)}, u32[]{:S(2)}, u32[]{:S(2)}) collective-permute-start(bf16[256,768]{1,0:T(8,128)(2,1)S(1)} %get-tuple-element.72), channel_id=1, source_target_pairs={{0,0},{1,1},{2,8},{3,9},{4,16},{5,17},{6,24},{7,25},{8,2},{9,3},{1... | collective-permute-start | bytes 1179656 | tf_op jit(solution)/shard_map/ppermute | solution.py:71
  14.3 132.8 %collective-permute-start.13 = (bf16[512,768]{1,0:T(8,128)(2,1)}, bf16[512,768]{1,0:T(8,128)(2,1)S(1)}, u32[]{:S(2)}, u32[]{:S(2)}) collective-permute-start(bf16[512,768]{1,0:T(8,128)(2,1)} %bitcast.34), channel_id=1, source_target_pairs={{0,0},{1,1},{2,8},{3,9},{4,16},{5,17},{6,24},{7,25},{8,2},{9,3},{1... | collective-permute-start | bytes 2359304 | tf_op jit(solution)/shard_map/ppermute | solution.py:71
  17.7 131.1 %collective-permute-start.14 = (bf16[512,768]{1,0:T(8,128)(2,1)}, bf16[512,768]{1,0:T(8,128)(2,1)}, u32[]{:S(2)}, u32[]{:S(2)}) collective-permute-start(bf16[512,768]{1,0:T(8,128)(2,1)} %bitcast.34), channel_id=1, source_target_pairs={{0,2},{1,3},{2,10},{3,11},{4,18},{5,19},{6,26},{7,27},{8,0},{9,1},... | collective-permute-start | bytes 2359304 | tf_op jit(solution)/shard_map/ppermute | solution.py:71
  35.7 69.5 %collective-permute-start.6 = (bf16[256,768]{1,0:T(8,128)(2,1)S(1)}, bf16[256,768]{1,0:T(8,128)(2,1)S(1)}, u32[]{:S(2)}, u32[]{:S(2)}) collective-permute-start(bf16[256,768]{1,0:T(8,128)(2,1)S(1)} %get-tuple-element.72), channel_id=1, source_target_pairs={{0,2},{1,3},{2,10},{3,11},{4,18},{5,19},{6,26},{7,27},{8,0},{9,1},... | collective-permute-start | bytes 1179656 | tf_op jit(solution)/shard_map/ppermute | solution.py:71
  44.5 101.5 %collective-permute-start.7 = (bf16[256,768]{1,0:T(8,128)(2,1)S(1)}, bf16[256,768]{1,0:T(8,128)(2,1)S(1)}, u32[]{:S(2)}, u32[]{:S(2)}) collective-permute-start(bf16[256,768]{1,0:T(8,128)(2,1)S(1)} %get-tuple-element.72), channel_id=1, source_target_pairs={{0,4},{1,5},{2,12},{3,13},{4,20},{5,21},{6,28},{7,29},{8,6},{9,7},... | collective-permute-start | bytes 1179656 | tf_op jit(solution)/shard_map/ppermute | solution.py:71
  101.9 44.1 %collective-permute-start.8 = (bf16[256,768]{1,0:T(8,128)(2,1)S(1)}, bf16[256,768]{1,0:T(8,128)(2,1)S(1)}, u32[]{:S(2)}, u32[]{:S(2)}) collective-permute-start(bf16[256,768]{1,0:T(8,128)(2,1)S(1)} %get-tuple-element.72), channel_id=1, source_target_pairs={{0,6},{1,7},{2,14},{3,15},{4,22},{5,23},{6,30},{7,31},{8,4},{9,5},... | collective-permute-start | bytes 1179656 | tf_op jit(solution)/shard_map/ppermute | solution.py:71
  105.2 76.4 %collective-permute-start.15 = (bf16[512,768]{1,0:T(8,128)(2,1)}, bf16[512,768]{1,0:T(8,128)(2,1)}, u32[]{:S(2)}, u32[]{:S(2)}) collective-permute-start(bf16[512,768]{1,0:T(8,128)(2,1)} %bitcast.34), channel_id=1, source_target_pairs={{0,4},{1,5},{2,12},{3,13},{4,20},{5,21},{6,28},{7,29},{8,6},{9,7},... | collective-permute-start | bytes 2359304 | tf_op jit(solution)/shard_map/ppermute | solution.py:71
  146.0 72.0 %collective-permute-start.4 = (bf16[4,256,768]{2,1,0:T(8,128)(2,1)S(1)}, bf16[4,256,768]{2,1,0:T(8,128)(2,1)}, u32[]{:S(2)}, u32[]{:S(2)}) collective-permute-start(bf16[4,256,768]{2,1,0:T(8,128)(2,1)S(1)} %pad_maximum_fusion.1), channel_id=1, source_target_pairs={{0,1},{1,0},{2,3},{3,2},{4,5},{5,4},{6,7},{7,6},{8,9},{9,8},{10,11... | collective-permute-start | bytes 4718600 | tf_op jit(solution)/shard_map/ppermute | solution.py:24
  146.3 71.8 %collective-permute-start.9 = (bf16[4,256,768]{2,1,0:T(8,128)(2,1)S(1)}, bf16[4,256,768]{2,1,0:T(8,128)(2,1)}, u32[]{:S(2)}, u32[]{:S(2)}) collective-permute-start(bf16[4,256,768]{2,1,0:T(8,128)(2,1)S(1)} %pad_maximum_fusion.2), channel_id=1, source_target_pairs={{0,1},{1,0},{2,3},{3,2},{4,5},{5,4},{6,7},{7,6},{8,9},{9,8},{10,11... | collective-permute-start | bytes 4718600 | tf_op jit(solution)/shard_map/ppermute | solution.py:24
  183.7 93.6 %collective-permute-start.17 = (bf16[4,512,768]{2,1,0:T(8,128)(2,1)S(1)}, bf16[4,512,768]{2,1,0:T(8,128)(2,1)S(1)}, u32[]{:S(2)}, u32[]{:S(2)}) collective-permute-start(bf16[4,512,768]{2,1,0:T(8,128)(2,1)S(1)} %pad_maximum_fusion), channel_id=1, source_target_pairs={{0,1},{1,0},{2,3},{3,2},{4,5},{5,4},{6,7},{7,6},{8,9},{9,8},{10,11... | collective-permute-start | bytes 9437192 | tf_op jit(solution)/shard_map/ppermute | solution.py:24
  185.2 63.0 %collective-permute-start.11 = (f32[4,256,256]{2,1,0:T(8,128)S(1)}, f32[4,256,256]{2,1,0:T(8,128)S(1)}, u32[]{:S(2)}, u32[]{:S(2)}) collective-permute-start(f32[4,256,256]{2,1,0:T(8,128)S(1)} %fusion.46), channel_id=1, source_target_pairs={{0,2},{1,3},{2,0},{3,1},{4,6},{5,7},{6,4},{7,5},{8,10},{9,11},{10,... | collective-permute-start | bytes 3145736 | tf_op jit(solution)/shard_map/ppermute | solution.py:24
  229.6 38.0 %collective-permute-start.28 = (bf16[256,3072]{1,0:T(8,128)(2,1)}, bf16[256,3072]{1,0:T(8,128)(2,1)}, u32[]{:S(2)}, u32[]{:S(2)}) collective-permute-start(bf16[256,3072]{1,0:T(8,128)(2,1)} %convolution_convert_fusion.1), channel_id=1, source_target_pairs={{0,16},{8,24},{16,0},{24,8},{1,17},{9,25},{17,1},{25,9},{2,18},{10... | collective-permute-start | bytes 4718600 | tf_op jit(solution)/shard_map/ppermute | solution.py:19
  239.7 107.8 %collective-permute-start.27 = (bf16[256,3072]{1,0:T(8,128)(2,1)}, bf16[256,3072]{1,0:T(8,128)(2,1)}, u32[]{:S(2)}, u32[]{:S(2)}) collective-permute-start(bf16[256,3072]{1,0:T(8,128)(2,1)} %convolution_convert_fusion.2), channel_id=1, source_target_pairs={{0,16},{8,24},{16,0},{24,8},{1,17},{9,25},{17,1},{25,9},{2,18},{10... | collective-permute-start | bytes 4718600 | tf_op jit(solution)/shard_map/ppermute | solution.py:19
  248.2 101.0 %collective-permute-start.21 = (bf16[256,3072]{1,0:T(8,128)(2,1)}, bf16[256,3072]{1,0:T(8,128)(2,1)}, u32[]{:S(2)}, u32[]{:S(2)}) collective-permute-start(bf16[256,3072]{1,0:T(8,128)(2,1)} %convolution_convert_fusion.4), channel_id=1, source_target_pairs={{0,8},{8,0},{16,24},{24,16},{1,9},{9,1},{17,25},{25,17},{2,10},{10... | collective-permute-start | bytes 4718600 | tf_op jit(solution)/shard_map/ppermute | solution.py:19
  267.6 78.0 %collective-permute-start.12 = (f32[4,256,256]{2,1,0:T(8,128)S(1)}, f32[4,256,256]{2,1,0:T(8,128)S(1)}, u32[]{:S(2)}, u32[]{:S(2)}) collective-permute-start(f32[4,256,256]{2,1,0:T(8,128)S(1)} %fusion.97), channel_id=1, source_target_pairs={{0,4},{1,5},{2,6},{3,7},{4,0},{5,1},{6,2},{7,3},{8,12},{9,13},{10,... | collective-permute-start | bytes 3145736 | tf_op jit(solution)/shard_map/ppermute | solution.py:24
  291.2 49.0 %collective-permute-start.19 = (bf16[256,3072]{1,0:T(8,128)(2,1)}, bf16[256,3072]{1,0:T(8,128)(2,1)}, u32[]{:S(2)}, u32[]{:S(2)}) collective-permute-start(bf16[256,3072]{1,0:T(8,128)(2,1)} %get-tuple-element.55), channel_id=1, source_target_pairs={{0,8},{8,0},{16,24},{24,16},{1,9},{9,1},{17,25},{25,17},{2,10},{10... | collective-permute-start | bytes 4718600 | tf_op jit(solution)/shard_map/ppermute | solution.py:19
  294.8 48.7 %collective-permute-start.25 = (bf16[256,3072]{1,0:T(8,128)(2,1)}, bf16[256,3072]{1,0:T(8,128)(2,1)}, u32[]{:S(2)}, u32[]{:S(2)}) collective-permute-start(bf16[256,3072]{1,0:T(8,128)(2,1)} %get-tuple-element.54), channel_id=1, source_target_pairs={{0,16},{8,24},{16,0},{24,8},{1,17},{9,25},{17,1},{25,9},{2,18},{10... | collective-permute-start | bytes 4718600 | tf_op jit(solution)/shard_map/ppermute | solution.py:19
  343.5 44.3 %collective-permute-start.23 = (bf16[256,3072]{1,0:T(8,128)(2,1)}, bf16[256,3072]{1,0:T(8,128)(2,1)S(1)}, u32[]{:S(2)}, u32[]{:S(2)}) collective-permute-start(bf16[256,3072]{1,0:T(8,128)(2,1)} %add_convert_fusion.1), channel_id=1, source_target_pairs={{0,16},{8,24},{16,0},{24,8},{1,17},{9,25},{17,1},{25,9},{2,18},{10... | collective-permute-start | bytes 4718600 | tf_op jit(solution)/shard_map/ppermute | solution.py:19
  345.7 65.6 %collective-permute-start.18 = (bf16[256,3072]{1,0:T(8,128)(2,1)S(1)}, bf16[256,3072]{1,0:T(8,128)(2,1)}, u32[]{:S(2)}, u32[]{:S(2)}) collective-permute-start(bf16[256,3072]{1,0:T(8,128)(2,1)S(1)} %slice.163), channel_id=1, source_target_pairs={{0,8},{8,0},{16,24},{24,16},{1,9},{9,1},{17,25},{25,17},{2,10},{10... | collective-permute-start | bytes 4718600 | tf_op jit(solution)/shard_map/ppermute | solution.py:19
  347.5 67.3 %collective-permute-start.24 = (bf16[256,3072]{1,0:T(8,128)(2,1)S(1)}, bf16[256,3072]{1,0:T(8,128)(2,1)}, u32[]{:S(2)}, u32[]{:S(2)}) collective-permute-start(bf16[256,3072]{1,0:T(8,128)(2,1)S(1)} %slice.162), channel_id=1, source_target_pairs={{0,16},{8,24},{16,0},{24,8},{1,17},{9,25},{17,1},{25,9},{2,18},{10... | collective-permute-start | bytes 4718600 | tf_op jit(solution)/shard_map/ppermute | solution.py:19
  349.2 97.6 %collective-permute-start.20 = (bf16[256,3072]{1,0:T(8,128)(2,1)}, bf16[256,3072]{1,0:T(8,128)(2,1)}, u32[]{:S(2)}, u32[]{:S(2)}) collective-permute-start(bf16[256,3072]{1,0:T(8,128)(2,1)} %fusion.22), channel_id=1, source_target_pairs={{0,16},{8,24},{16,0},{24,8},{1,17},{9,25},{17,1},{25,9},{2,18},{10... | collective-permute-start | bytes 4718600 | tf_op jit(solution)/shard_map/ppermute | solution.py:19
  377.4 69.5 %collective-permute-start.26 = (bf16[256,3072]{1,0:T(8,128)(2,1)S(1)}, bf16[256,3072]{1,0:T(8,128)(2,1)}, u32[]{:S(2)}, u32[]{:S(2)}) collective-permute-start(bf16[256,3072]{1,0:T(8,128)(2,1)S(1)} %fusion.20), channel_id=1, source_target_pairs={{0,8},{8,0},{16,24},{24,16},{1,9},{9,1},{17,25},{25,17},{2,10},{10... | collective-permute-start | bytes 4718600 | tf_op jit(solution)/shard_map/ppermute | solution.py:19
  479.3 105.6 %collective-permute-start.35 = (bf16[256,3072]{1,0:T(8,128)(2,1)}, bf16[256,3072]{1,0:T(8,128)(2,1)}, u32[]{:S(2)}, u32[]{:S(2)}) collective-permute-start(bf16[256,3072]{1,0:T(8,128)(2,1)} %get-tuple-element.41), channel_id=1, source_target_pairs={{0,16},{8,24},{16,0},{24,8},{1,17},{9,25},{17,1},{25,9},{2,18},{10... | collective-permute-start | bytes 4718600 | tf_op jit(solution)/shard_map/ppermute | solution.py:19
  483.2 66.5 %collective-permute-start.34 = (bf16[256,3072]{1,0:T(8,128)(2,1)}, bf16[256,3072]{1,0:T(8,128)(2,1)}, u32[]{:S(2)}, u32[]{:S(2)}) collective-permute-start(bf16[256,3072]{1,0:T(8,128)(2,1)} %get-tuple-element.39), channel_id=1, source_target_pairs={{0,8},{8,0},{16,24},{24,16},{1,9},{9,1},{17,25},{25,17},{2,10},{10... | collective-permute-start | bytes 4718600 | tf_op jit(solution)/shard_map/ppermute | solution.py:19
  484.7 103.4 %collective-permute-start.36 = (bf16[256,3072]{1,0:T(8,128)(2,1)}, bf16[256,3072]{1,0:T(8,128)(2,1)}, u32[]{:S(2)}, u32[]{:S(2)}) collective-permute-start(bf16[256,3072]{1,0:T(8,128)(2,1)} %get-tuple-element.39), channel_id=1, source_target_pairs={{0,16},{8,24},{16,0},{24,8},{1,17},{9,25},{17,1},{25,9},{2,18},{10... | collective-permute-start | bytes 4718600 | tf_op jit(solution)/shard_map/ppermute | solution.py:19
  489.3 94.1 %collective-permute-start.42 = (bf16[256,3072]{1,0:T(8,128)(2,1)}, bf16[256,3072]{1,0:T(8,128)(2,1)}, u32[]{:S(2)}, u32[]{:S(2)}) collective-permute-start(bf16[256,3072]{1,0:T(8,128)(2,1)} %get-tuple-element.37), channel_id=1, source_target_pairs={{0,8},{8,0},{16,24},{24,16},{1,9},{9,1},{17,25},{25,17},{2,10},{10... | collective-permute-start | bytes 4718600 | tf_op jit(solution)/shard_map/ppermute | solution.py:19
  516.0 110.7 %collective-permute-start.44 = (bf16[256,3072]{1,0:T(8,128)(2,1)}, bf16[256,3072]{1,0:T(8,128)(2,1)S(1)}, u32[]{:S(2)}, u32[]{:S(2)}) collective-permute-start(bf16[256,3072]{1,0:T(8,128)(2,1)} %get-tuple-element.37), channel_id=1, source_target_pairs={{0,16},{8,24},{16,0},{24,8},{1,17},{9,25},{17,1},{25,9},{2,18},{10... | collective-permute-start | bytes 4718600 | tf_op jit(solution)/shard_map/ppermute | solution.py:19
  549.7 74.6 %collective-permute-start.43 = (bf16[256,3072]{1,0:T(8,128)(2,1)S(1)}, bf16[256,3072]{1,0:T(8,128)(2,1)S(1)}, u32[]{:S(2)}, u32[]{:S(2)}) collective-permute-start(bf16[256,3072]{1,0:T(8,128)(2,1)S(1)} %get-tuple-element.35), channel_id=1, source_target_pairs={{0,8},{8,0},{16,24},{24,16},{1,9},{9,1},{17,25},{25,17},{2,10},{10... | collective-permute-start | bytes 4718600 | tf_op jit(solution)/shard_map/ppermute | solution.py:19
  584.9 69.5 %collective-permute-start.46 = (bf16[256,3072]{1,0:T(8,128)(2,1)}, bf16[256,3072]{1,0:T(8,128)(2,1)S(1)}, u32[]{:S(2)}, u32[]{:S(2)}) collective-permute-start(bf16[256,3072]{1,0:T(8,128)(2,1)} %collective-permute-done.42), channel_id=1, source_target_pairs={{0,16},{8,24},{16,0},{24,8},{1,17},{9,25},{17,1},{25,9},{2,18},{10... | collective-permute-start | bytes 4718600 | tf_op jit(solution)/shard_map/ppermute | solution.py:19
  611.3 97.3 %collective-permute-start.38 = (bf16[256,3072]{1,0:T(8,128)(2,1)}, bf16[256,3072]{1,0:T(8,128)(2,1)S(1)}, u32[]{:S(2)}, u32[]{:S(2)}) collective-permute-start(bf16[256,3072]{1,0:T(8,128)(2,1)} %collective-permute-done.36), channel_id=1, source_target_pairs={{0,8},{8,0},{16,24},{24,16},{1,9},{9,1},{17,25},{25,17},{2,10},{10... | collective-permute-start | bytes 4718600 | tf_op jit(solution)/shard_map/ppermute | solution.py:19
  620.7 60.6 %collective-permute-start.47 = (bf16[256,3072]{1,0:T(8,128)(2,1)S(1)}, bf16[256,3072]{1,0:T(8,128)(2,1)S(1)}, u32[]{:S(2)}, u32[]{:S(2)}) collective-permute-start(bf16[256,3072]{1,0:T(8,128)(2,1)S(1)} %collective-permute-done.45), channel_id=1, source_target_pairs={{0,8},{8,0},{16,24},{24,16},{1,9},{9,1},{17,25},{25,17},{2,10},{10... | collective-permute-start | bytes 4718600 | tf_op jit(solution)/shard_map/ppermute | solution.py:19
  624.3 84.3 %collective-permute-start.37 = (bf16[256,3072]{1,0:T(8,128)(2,1)}, bf16[256,3072]{1,0:T(8,128)(2,1)S(1)}, u32[]{:S(2)}, u32[]{:S(2)}) collective-permute-start(bf16[256,3072]{1,0:T(8,128)(2,1)} %collective-permute-done.33), channel_id=1, source_target_pairs={{0,16},{8,24},{16,0},{24,8},{1,17},{9,25},{17,1},{25,9},{2,18},{10... | collective-permute-start | bytes 4718600 | tf_op jit(solution)/shard_map/ppermute | solution.py:19
  (45 other events, 1160.8 us)

commit v2 on v1

--- a/solution.py
+++ b/solution.py
@@ -111,32 +111,35 @@
     x_rows, pre = [], []
     for a in range(images):
         x_rows.append(spread(inputs[a], groups))
-        partial = {r: rows_dot(x_rows[a][r], w_up) for r in order}
+        partial = {}
+        for r in order:
+            partial[r] = rows_dot(x_rows[a][r], w_up)
         pre.append(reduce_rows(partial, *routes[a]))
 
     y_rows = spread(cotangent.reshape(images * patches, feats), groups)
-    partial = {r: rows_dot_t(y_rows[r], w_down) for r in order}
-    dact = [
-        reduce_rows([partial[r][image[a]] for r in range(groups)], *routes[a])
-        for a in range(images)
-    ]
+    partial = {}
+    for r in order:
+        partial[r] = rows_dot_t(y_rows[r], w_down)
+    dact = [reduce_rows([partial[r][image[a]] for r in range(groups)], *routes[a]) for a in range(images)]
     own = [inputs[a] for a in range(images)] + [cotangent[a] for a in range(images)]
     grams = sum_mp(jnp.stack([gram(rows) for rows in own]))
 
-    def clip(rows, grams_of, which):
+    def clip(rows, grams_of, thresholds, which):
         part = jnp.stack([jnp.sum(grams_of[a] * gram(rows[a])) for a in range(images)])
         norms = jnp.sqrt(sum_mp(part))
         factor = jnp.minimum(1.0, thresholds[which] / (norms + 1e-06))
         return [(factor[a] * rows[a].astype(f32)).astype(bf16) for a in range(images)], norms
 
     act = [(p * normal_cdf(p)).astype(bf16) for p in pre]
-    act_clip, norms_down = clip(act, grams[images:], 1)
+    pre, act = lax.optimization_barrier((pre, act))
+    act_clip, norms_down = clip(act, grams[images:], thresholds, 1)
     act_rows = [gather_rows(act_clip[a], *routes[a]) for a in range(images)]
     dpre = [
         (d * (normal_cdf(p) + p * jnp.exp(-0.5 * p * p) * inv_root_two_pi)).astype(bf16)
         for p, d in zip(pre, dact)
     ]
-    dpre_clip, norms_up = clip(dpre, grams[:images], 0)
+    dpre, grams, thresholds, norms_down = lax.optimization_barrier((dpre, grams, thresholds, norms_down))
+    dpre_clip, norms_up = clip(dpre, grams[:images], thresholds, 0)
     dpre_rows = [gather_rows(dpre_clip[a], *routes[a]) for a in range(images)]
 
     def flat(wanted):

time: 725 us -> 678 us (0.935)
  waiting for transfers between devices: 311 us -> 263 us
  matrix products: 132 us -> 147 us
  starting transfers between devices: 204 us -> 190 us
    ppermute x24, waiting for transfers between devices: 275 us -> 174 us  [shift_dp(): return lax.ppermute(value, 'dp', [(g, g ^ flip) for g in range(count)])]
    ppermute x12, waiting for transfers between devices: 3.68 us -> 57.3 us  [swap_mp(): return lax.ppermute(value, 'mp', [(m, m ^ flip) for m in range(count)])]
    ppermute x12, starting transfers between devices: 140 us -> 123 us  [spread(): found.append(lax.ppermute(block, ('dp', 'mp'), pairs))]
    dot_general x8, matrix products: 31.2 us -> 44.4 us  [rows_dot(): return jnp.dot(left, right, preferred_element_type=f32)]
    unnamed x72 -> x66, local copies, waits for them, and re-layouts: 19.8 us -> 18.8 us
  transfers between devices with their start and end apart: 48 -> 48, of which waited for: 17 -> 19; matrix products, arithmetic and copies ran while one was open for 25% -> 30% of each run, Pallas kernels for 0% -> 0%
where the time goes in v2:
time: 678 us; the launch traced here: 675 us
  waiting for transfers between devices  263 us (39%)
  starting transfers between devices  190 us (28%)
  matrix products  147 us (22%)
  other arithmetic  44 us (6%)
  local copies, waits for them, and re-layouts  29.1 us (4%)
    ppermute x24, waiting for transfers between devices, shift_dp(): return lax.ppermute(value, 'dp', [(g, g ^ flip) for g in range(count)])  174 us
    ppermute x12, starting transfers between devices, spread(): found.append(lax.ppermute(block, ('dp', 'mp'), pairs))  123 us
    dot_general x3, matrix products, outer_dot(): lax.dot_general(left, right, (((0,), (0,)), ((), ())), preferred_element_...  61 us
    ppermute x12, waiting for transfers between devices, swap_mp(): return lax.ppermute(value, 'mp', [(m, m ^ flip) for m in range(count)])  57.3 us
    dot_general x8, matrix products, rows_dot(): return jnp.dot(left, right, preferred_element_type=f32)  44.4 us
    dot_general x12, matrix products, rows_dot_t(): lax.dot_general(left, right, (((1,), (1,)), ((), ())), preferred_element_...  41.6 us
    ppermute x12, starting transfers between devices, swap_mp(): return lax.ppermute(value, 'mp', [(m, m ^ flip) for m in range(count)])  36 us
    ppermute x12, waiting for transfers between devices, spread(): found.append(lax.ppermute(block, ('dp', 'mp'), pairs))  31.6 us
  transfers between devices with their start and end apart: 48, of which 19 were waited for; matrix products, arithmetic and copies ran while one was open for 30% of the time, Pallas kernels for 0%

profile of v2, /device:TPU:0, one launch (start us, length us, event | category | flops | bytes accessed | tf_op | source)
XLA Modules:
  0.0 674.9 jit_solution(16463387917894344814)
XLA Ops:
  2.5 5.7 collective-permute-start.1
  17.7 17.9 %collective-permute-start.6 = (bf16[256,768]{1,0:T(8,128)(2,1)S(1)}, bf16[256,768]{1,0:T(8,128)(2,1)S(1)}, u32[]{:S(2)}, u32[]{:S(2)}) collective-permute-start(bf16[256,768]{1,0:T(8,128)(2,1)S(1)} %get-tuple-element.92), channel_id=1, source_target_pairs={{0,2},{1,3},{2,10},{3,11},{4,18},{5,19},{6,26},{7,27},{8,0},{9,1},... | collective-permute-start | bytes 1179656 | tf_op jit(solution)/shard_map/ppermute | solution.py:71
  35.7 39.6 %collective-permute-start.7 = (bf16[256,768]{1,0:T(8,128)(2,1)S(1)}, bf16[256,768]{1,0:T(8,128)(2,1)S(1)}, u32[]{:S(2)}, u32[]{:S(2)}) collective-permute-start(bf16[256,768]{1,0:T(8,128)(2,1)S(1)} %get-tuple-element.92), channel_id=1, source_target_pairs={{0,4},{1,5},{2,12},{3,13},{4,20},{5,21},{6,28},{7,29},{8,6},{9,7},... | collective-permute-start | bytes 1179656 | tf_op jit(solution)/shard_map/ppermute | solution.py:71
  81.4 47.7 %collective-permute-start.12 = (bf16[512,768]{1,0:T(8,128)(2,1)}, bf16[512,768]{1,0:T(8,128)(2,1)}, u32[]{:S(2)}, u32[]{:S(2)}) collective-permute-start(bf16[512,768]{1,0:T(8,128)(2,1)} %bitcast.26), channel_id=1, source_target_pairs={{0,4},{1,5},{2,12},{3,13},{4,20},{5,21},{6,28},{7,29},{8,6},{9,7},... | collective-permute-start | bytes 2359304 | tf_op jit(solution)/shard_map/ppermute | solution.py:71
  132.6 31.3 %collective-permute-done.12 = bf16[512,768]{1,0:T(8,128)(2,1)} collective-permute-done((bf16[512,768]{1,0:T(8,128)(2,1)}, bf16[512,768]{1,0:T(8,128)(2,1)}, u32[]{:S(2)}, u32[]{:S(2)}) %collective-permute-start.12) | collective-permute-done | bytes 786464 | tf_op jit(solution)/shard_map/ppermute | solution.py:71
  167.8 32.5 %collective-permute-start.28 = (f32[4,256,256]{2,1,0:T(8,128)S(1)}, f32[4,256,256]{2,1,0:T(8,128)S(1)}, u32[]{:S(2)}, u32[]{:S(2)}) collective-permute-start(f32[4,256,256]{2,1,0:T(8,128)S(1)} %fusion.43), channel_id=1, source_target_pairs={{0,2},{1,3},{2,0},{3,1},{4,6},{5,7},{6,4},{7,5},{8,10},{9,11},{10,... | collective-permute-start | bytes 3145736 | tf_op jit(solution)/shard_map/ppermute | solution.py:24
  205.6 4.3 collective-permute-start.22
  209.9 3.9 convolution_convert_fusion.2
  213.8 5.2 fusion.51
  219.2 6.3 convolution_convert_fusion.3
  225.8 7.7 %convolution_convert_fusion.4 = bf16[256,3072]{1,0:T(8,128)(2,1)} fusion(bf16[256,1536]{1,0:T(8,128)(2,1)S(1)} %pad_maximum_fusion.9, bf16[1536,3072]{1,0:T(8,128)(2,1)} %param.7), kind=kOutput, calls=%fused_computation.15 | convolution fusion | flops 2416705536 | bytes 11796480 | tf_op jit(solution)/shard_map/dot_general | solution.py:36
  237.9 6.9 %fusion.50 = f32[256,3072]{1,0:T(8,128)S(1)} fusion(bf16[256,1536]{1,0:T(8,128)(2,1)S(1)} %pad_maximum_fusion.8, bf16[1536,3072]{1,0:T(8,128)(2,1)} %param.7), kind=kOutput, calls=%fused_computation.151 | convolution fusion | flops 2415919104 | bytes 13369344 | tf_op jit(solution)/shard_map/dot_general | solution.py:36
  244.8 38.9 %collective-permute-done.29 = f32[4,256,256]{2,1,0:T(8,128)S(1)} collective-permute-done((f32[4,256,256]{2,1,0:T(8,128)S(1)}, f32[4,256,256]{2,1,0:T(8,128)S(1)}, u32[]{:S(2)}, u32[]{:S(2)}) %collective-permute-start.29) | collective-permute-done | bytes 1048608 | tf_op jit(solution)/shard_map/ppermute | solution.py:24
  285.6 8.1 %add_convert_fusion = bf16[256,3072]{1,0:T(8,128)(2,1)} fusion(bf16[256,3072]{1,0:T(8,128)(2,1)S(1)} %collective-permute-done.22, bf16[256,1536]{1,0:T(8,128)(2,1)S(1)} %pad_maximum_fusion.13, bf16[1536,3072]{1,0:T(8,128)(2,1)} %param.7), kind=kOutput, calls=%fused_computation.49 | convolution fusion | flops 2418278400 | bytes 13369344 | tf_op jit(solution)/shard_map/dot_general | solution.py:36
  294.0 3.8 add_convert_fusion.1
  302.9 9.7 %convolution_convert_fusion = bf16[512,3072]{1,0:T(8,128)(2,1)S(1)} fusion(bf16[512,1536]{1,0:T(8,128)(2,1)S(1)} %get-tuple-element.33, bf16[3072,1536]{1,0:T(8,128)(2,1)} %param.8), kind=kOutput, calls=%fused_computation.11 | convolution fusion | flops 4833411072 | bytes 14155776 | tf_op jit(solution)/shard_map/dot_general | solution.py:40
  316.2 7.7 %fusion.48 = f32[512,3072]{1,0:T(8,128)S(1)} fusion(bf16[512,1536]{1,0:T(8,128)(2,1)S(1)} %get-tuple-element.31, bf16[3072,1536]{1,0:T(8,128)(2,1)} %param.8), kind=kOutput, calls=%fused_computation.149 | convolution fusion | flops 4831838208 | bytes 17301504 | tf_op jit(solution)/shard_map/dot_general | solution.py:40
  325.9 7.7 %fusion.49 = f32[512,3072]{1,0:T(8,128)S(1)} fusion(bf16[512,1536]{1,0:T(8,128)(2,1)S(1)} %copy-done.12, bf16[3072,1536]{1,0:T(8,128)(2,1)} %param.8), kind=kOutput, calls=%fused_computation.150 | convolution fusion | flops 4831838208 | bytes 17301504 | tf_op jit(solution)/shard_map/dot_general | solution.py:40
  334.1 20.8 %collective-permute-done.23 = bf16[256,3072]{1,0:T(8,128)(2,1)} collective-permute-done((bf16[256,3072]{1,0:T(8,128)(2,1)}, bf16[256,3072]{1,0:T(8,128)(2,1)}, u32[]{:S(2)}, u32[]{:S(2)}) %collective-permute-start.23) | collective-permute-done | bytes 1572896 | tf_op jit(solution)/shard_map/ppermute | solution.py:19
  367.6 3.6 collective-permute-done.31
  372.5 4.5 collective-permute-done.32
  384.4 4.3 collective-permute-done.16
  395.6 60.5 %collective-permute-done.42 = bf16[256,3072]{1,0:T(8,128)(2,1)} collective-permute-done((bf16[256,3072]{1,0:T(8,128)(2,1)S(1)}, bf16[256,3072]{1,0:T(8,128)(2,1)}, u32[]{:S(2)}, u32[]{:S(2)}) %collective-permute-start.42) | collective-permute-done | bytes 1572896 | tf_op jit(solution)/shard_map/ppermute | solution.py:19
  457.8 30.5 %collective-permute-done.43 = bf16[256,3072]{1,0:T(8,128)(2,1)S(1)} collective-permute-done((bf16[256,3072]{1,0:T(8,128)(2,1)S(1)}, bf16[256,3072]{1,0:T(8,128)(2,1)S(1)}, u32[]{:S(2)}, u32[]{:S(2)}) %collective-permute-start.43) | collective-permute-done | bytes 1572896 | tf_op jit(solution)/shard_map/ppermute | solution.py:19
  491.8 7.7 %fusion.47 = f32[512,3072]{1,0:T(8,128)S(1)} fusion(bf16[512,1536]{1,0:T(8,128)(2,1)S(1)} %copy-done.8, bf16[3072,1536]{1,0:T(8,128)(2,1)} %param.8), kind=kOutput, calls=%fused_computation.148 | convolution fusion | flops 4831838208 | bytes 17301504 | tf_op jit(solution)/shard_map/dot_general | solution.py:40
  507.9 17.9 %collective-permute-done.17 = bf16[256,3072]{1,0:T(8,128)(2,1)S(1)} collective-permute-done((bf16[256,3072]{1,0:T(8,128)(2,1)}, bf16[256,3072]{1,0:T(8,128)(2,1)S(1)}, u32[]{:S(2)}, u32[]{:S(2)}) %collective-permute-start.17) | collective-permute-done | bytes 1572896 | tf_op jit(solution)/shard_map/ppermute | solution.py:19
  527.4 4.6 fusion.19
  543.3 4.5 collective-permute-done.35
  566.8 26.1 %fusion = f32[3072,1536]{1,0:T(8,128)} fusion(bf16[2048,3072]{1,0:T(8,128)(2,1)} %constant_dynamic-update-slice_fusion.12, bf16[512,1536]{1,0:T(8,128)(2,1)S(1)} %copy-done.15, bf16[512,1536]{1,0:T(8,128)(2,1)S(1)} %copy-done.13, bf16[512,1536]{1,0:T(8,128)(2,1)S(1)} %copy-done.11, bf16[512,1536]{1,0:T(8,128)(2,1)S(1)} %copy-done.9), kind=kOutput, calls=%fused_computation.1 | convolution fusion | flops 19352518656 | bytes 37748736 | tf_op jit(solution)/shard_map/dot_general | solution.py:44
  592.9 32.1 %collective-permute-done.39 = bf16[256,3072]{1,0:T(8,128)(2,1)S(1)} collective-permute-done((bf16[256,3072]{1,0:T(8,128)(2,1)S(1)}, bf16[256,3072]{1,0:T(8,128)(2,1)S(1)}, u32[]{:S(2)}, u32[]{:S(2)}) %collective-permute-start.39) | collective-permute-done | bytes 1572896 | tf_op jit(solution)/shard_map/ppermute | solution.py:19
  636.4 21.4 %fusion.53 = f32[1536,3072]{1,0:T(8,128)} fusion(bf16[1536,1536]{1,0:T(8,128)(2,1)} %copy-done.18, bf16[1536,3072]{1,0:T(8,128)(2,1)} %constant_dynamic-update-slice_fusion.6), kind=kOutput, calls=%fused_computation.154 | convolution fusion | flops 14495514624 | bytes 33030144 | tf_op jit(solution)/shard_map/dot_general | solution.py:44
  660.9 13.5 %convolution_add_fusion = f32[1536,3072]{1,0:T(8,128)} fusion(f32[1536,3072]{1,0:T(8,128)} %fusion.53, bf16[256,3072]{1,0:T(8,128)(2,1)S(1)} %collective-permute-done.41, bf16[256,3072]{1,0:T(8,128)(2,1)S(1)} %collective-permute-done.40, bf16[256,1536]{1,0:T(8,128)(2,1)S(1)} %copy-done.1, bf16[256,1536]{1,0:T(8,128)(2,1)S(1)} %pad_maximum_fusion.11), kind=kOutput, calls=%fused_computation | convolution fusion | flops 4845993984 | bytes 42467328 | tf_op jit(solution)/shard_map/dot_general | solution.py:44
  (202 shorter events, 136.4 us)
Async XLA Ops:
  11.7 63.5 %collective-permute-start.3 = (bf16[256,768]{1,0:T(8,128)(2,1)S(1)}, bf16[256,768]{1,0:T(8,128)(2,1)S(1)}, u32[]{:S(2)}, u32[]{:S(2)}) collective-permute-start(bf16[256,768]{1,0:T(8,128)(2,1)S(1)} %get-tuple-element.93), channel_id=1, source_target_pairs={{0,6},{1,7},{2,14},{3,15},{4,22},{5,23},{6,30},{7,31},{8,4},{9,5},... | collective-permute-start | bytes 1179656 | tf_op jit(solution)/shard_map/ppermute | solution.py:71
  13.6 61.6 %collective-permute-start.5 = (bf16[256,768]{1,0:T(8,128)(2,1)S(1)}, bf16[256,768]{1,0:T(8,128)(2,1)S(1)}, u32[]{:S(2)}, u32[]{:S(2)}) collective-permute-start(bf16[256,768]{1,0:T(8,128)(2,1)S(1)} %get-tuple-element.92), channel_id=1, source_target_pairs={{0,0},{1,1},{2,8},{3,9},{4,16},{5,17},{6,24},{7,25},{8,2},{9,3},{1... | collective-permute-start | bytes 1179656 | tf_op jit(solution)/shard_map/ppermute | solution.py:71
  14.3 115.9 %collective-permute-start.10 = (bf16[512,768]{1,0:T(8,128)(2,1)}, bf16[512,768]{1,0:T(8,128)(2,1)S(1)}, u32[]{:S(2)}, u32[]{:S(2)}) collective-permute-start(bf16[512,768]{1,0:T(8,128)(2,1)} %bitcast.26), channel_id=1, source_target_pairs={{0,0},{1,1},{2,8},{3,9},{4,16},{5,17},{6,24},{7,25},{8,2},{9,3},{1... | collective-permute-start | bytes 2359304 | tf_op jit(solution)/shard_map/ppermute | solution.py:71
  17.7 63.7 %collective-permute-start.6 = (bf16[256,768]{1,0:T(8,128)(2,1)S(1)}, bf16[256,768]{1,0:T(8,128)(2,1)S(1)}, u32[]{:S(2)}, u32[]{:S(2)}) collective-permute-start(bf16[256,768]{1,0:T(8,128)(2,1)S(1)} %get-tuple-element.92), channel_id=1, source_target_pairs={{0,2},{1,3},{2,10},{3,11},{4,18},{5,19},{6,26},{7,27},{8,0},{9,1},... | collective-permute-start | bytes 1179656 | tf_op jit(solution)/shard_map/ppermute | solution.py:71
  35.7 93.5 %collective-permute-start.7 = (bf16[256,768]{1,0:T(8,128)(2,1)S(1)}, bf16[256,768]{1,0:T(8,128)(2,1)S(1)}, u32[]{:S(2)}, u32[]{:S(2)}) collective-permute-start(bf16[256,768]{1,0:T(8,128)(2,1)S(1)} %get-tuple-element.92), channel_id=1, source_target_pairs={{0,4},{1,5},{2,12},{3,13},{4,20},{5,21},{6,28},{7,29},{8,6},{9,7},... | collective-permute-start | bytes 1179656 | tf_op jit(solution)/shard_map/ppermute | solution.py:71
  75.2 53.9 %collective-permute-start.8 = (bf16[256,768]{1,0:T(8,128)(2,1)S(1)}, bf16[256,768]{1,0:T(8,128)(2,1)S(1)}, u32[]{:S(2)}, u32[]{:S(2)}) collective-permute-start(bf16[256,768]{1,0:T(8,128)(2,1)S(1)} %get-tuple-element.92), channel_id=1, source_target_pairs={{0,6},{1,7},{2,14},{3,15},{4,22},{5,23},{6,30},{7,31},{8,4},{9,5},... | collective-permute-start | bytes 1179656 | tf_op jit(solution)/shard_map/ppermute | solution.py:71
  75.2 56.7 %collective-permute-start.11 = (bf16[512,768]{1,0:T(8,128)(2,1)}, bf16[512,768]{1,0:T(8,128)(2,1)}, u32[]{:S(2)}, u32[]{:S(2)}) collective-permute-start(bf16[512,768]{1,0:T(8,128)(2,1)} %bitcast.26), channel_id=1, source_target_pairs={{0,2},{1,3},{2,10},{3,11},{4,18},{5,19},{6,26},{7,27},{8,0},{9,1},... | collective-permute-start | bytes 2359304 | tf_op jit(solution)/shard_map/ppermute | solution.py:71
  81.4 82.6 %collective-permute-start.12 = (bf16[512,768]{1,0:T(8,128)(2,1)}, bf16[512,768]{1,0:T(8,128)(2,1)}, u32[]{:S(2)}, u32[]{:S(2)}) collective-permute-start(bf16[512,768]{1,0:T(8,128)(2,1)} %bitcast.26), channel_id=1, source_target_pairs={{0,4},{1,5},{2,12},{3,13},{4,20},{5,21},{6,28},{7,29},{8,6},{9,7},... | collective-permute-start | bytes 2359304 | tf_op jit(solution)/shard_map/ppermute | solution.py:71
  129.1 71.2 %collective-permute-start.4 = (bf16[4,256,768]{2,1,0:T(8,128)(2,1)S(1)}, bf16[4,256,768]{2,1,0:T(8,128)(2,1)}, u32[]{:S(2)}, u32[]{:S(2)}) collective-permute-start(bf16[4,256,768]{2,1,0:T(8,128)(2,1)S(1)} %pad_maximum_fusion.1), channel_id=1, source_target_pairs={{0,1},{1,0},{2,3},{3,2},{4,5},{5,4},{6,7},{7,6},{8,9},{9,8},{10,11... | collective-permute-start | bytes 4718600 | tf_op jit(solution)/shard_map/ppermute | solution.py:24
  129.3 70.9 %collective-permute-start.9 = (bf16[4,256,768]{2,1,0:T(8,128)(2,1)S(1)}, bf16[4,256,768]{2,1,0:T(8,128)(2,1)}, u32[]{:S(2)}, u32[]{:S(2)}) collective-permute-start(bf16[4,256,768]{2,1,0:T(8,128)(2,1)S(1)} %pad_maximum_fusion.2), channel_id=1, source_target_pairs={{0,1},{1,0},{2,3},{3,2},{4,5},{5,4},{6,7},{7,6},{8,9},{9,8},{10,11... | collective-permute-start | bytes 4718600 | tf_op jit(solution)/shard_map/ppermute | solution.py:24
  166.1 133.4 %collective-permute-start.14 = (bf16[4,512,768]{2,1,0:T(8,128)(2,1)S(1)}, bf16[4,512,768]{2,1,0:T(8,128)(2,1)S(1)}, u32[]{:S(2)}, u32[]{:S(2)}) collective-permute-start(bf16[4,512,768]{2,1,0:T(8,128)(2,1)S(1)} %pad_maximum_fusion), channel_id=1, source_target_pairs={{0,1},{1,0},{2,3},{3,2},{4,5},{5,4},{6,7},{7,6},{8,9},{9,8},{10,11... | collective-permute-start | bytes 9437192 | tf_op jit(solution)/shard_map/ppermute | solution.py:24
  167.8 65.8 %collective-permute-start.28 = (f32[4,256,256]{2,1,0:T(8,128)S(1)}, f32[4,256,256]{2,1,0:T(8,128)S(1)}, u32[]{:S(2)}, u32[]{:S(2)}) collective-permute-start(f32[4,256,256]{2,1,0:T(8,128)S(1)} %fusion.43), channel_id=1, source_target_pairs={{0,2},{1,3},{2,0},{3,1},{4,6},{5,7},{6,4},{7,5},{8,10},{9,11},{10,... | collective-permute-start | bytes 3145736 | tf_op jit(solution)/shard_map/ppermute | solution.py:24
  205.6 80.0 %collective-permute-start.22 = (bf16[256,3072]{1,0:T(8,128)(2,1)S(1)}, bf16[256,3072]{1,0:T(8,128)(2,1)S(1)}, u32[]{:S(2)}, u32[]{:S(2)}) collective-permute-start(bf16[256,3072]{1,0:T(8,128)(2,1)S(1)} %convolution_convert_fusion.1), channel_id=1, source_target_pairs={{0,16},{8,24},{16,0},{24,8},{1,17},{9,25},{17,1},{25,9},{2,18},{10... | collective-permute-start | bytes 4718600 | tf_op jit(solution)/shard_map/ppermute | solution.py:19
  213.7 120.0 %collective-permute-start.21 = (bf16[256,3072]{1,0:T(8,128)(2,1)}, bf16[256,3072]{1,0:T(8,128)(2,1)}, u32[]{:S(2)}, u32[]{:S(2)}) collective-permute-start(bf16[256,3072]{1,0:T(8,128)(2,1)} %convolution_convert_fusion.2), channel_id=1, source_target_pairs={{0,16},{8,24},{16,0},{24,8},{1,17},{9,25},{17,1},{25,9},{2,18},{10... | collective-permute-start | bytes 4718600 | tf_op jit(solution)/shard_map/ppermute | solution.py:19
  225.5 68.5 %collective-permute-start.19 = (bf16[256,3072]{1,0:T(8,128)(2,1)S(1)}, bf16[256,3072]{1,0:T(8,128)(2,1)S(1)}, u32[]{:S(2)}, u32[]{:S(2)}) collective-permute-start(bf16[256,3072]{1,0:T(8,128)(2,1)S(1)} %convolution_convert_fusion.3), channel_id=1, source_target_pairs={{0,8},{8,0},{16,24},{24,16},{1,9},{9,1},{17,25},{25,17},{2,10},{10... | collective-permute-start | bytes 4718600 | tf_op jit(solution)/shard_map/ppermute | solution.py:19
  235.0 48.7 %collective-permute-start.29 = (f32[4,256,256]{2,1,0:T(8,128)S(1)}, f32[4,256,256]{2,1,0:T(8,128)S(1)}, u32[]{:S(2)}, u32[]{:S(2)}) collective-permute-start(f32[4,256,256]{2,1,0:T(8,128)S(1)} %fusion.91), channel_id=1, source_target_pairs={{0,4},{1,5},{2,6},{3,7},{4,0},{5,1},{6,2},{7,3},{8,12},{9,13},{10,... | collective-permute-start | bytes 3145736 | tf_op jit(solution)/shard_map/ppermute | solution.py:24
  283.7 75.5 %collective-permute-start.18 = (bf16[256,3072]{1,0:T(8,128)(2,1)}, bf16[256,3072]{1,0:T(8,128)(2,1)}, u32[]{:S(2)}, u32[]{:S(2)}) collective-permute-start(bf16[256,3072]{1,0:T(8,128)(2,1)} %convolution_convert_fusion.4), channel_id=1, source_target_pairs={{0,8},{8,0},{16,24},{24,16},{1,9},{9,1},{17,25},{25,17},{2,10},{10... | collective-permute-start | bytes 4718600 | tf_op jit(solution)/shard_map/ppermute | solution.py:19
  293.7 61.3 %collective-permute-start.23 = (bf16[256,3072]{1,0:T(8,128)(2,1)}, bf16[256,3072]{1,0:T(8,128)(2,1)}, u32[]{:S(2)}, u32[]{:S(2)}) collective-permute-start(bf16[256,3072]{1,0:T(8,128)(2,1)} %add_convert_fusion), channel_id=1, source_target_pairs={{0,8},{8,0},{16,24},{24,16},{1,9},{9,1},{17,25},{25,17},{2,10},{10... | collective-permute-start | bytes 4718600 | tf_op jit(solution)/shard_map/ppermute | solution.py:19
  297.8 61.4 %collective-permute-start.20 = (bf16[256,3072]{1,0:T(8,128)(2,1)}, bf16[256,3072]{1,0:T(8,128)(2,1)}, u32[]{:S(2)}, u32[]{:S(2)}) collective-permute-start(bf16[256,3072]{1,0:T(8,128)(2,1)} %add_convert_fusion.1), channel_id=1, source_target_pairs={{0,16},{8,24},{16,0},{24,8},{1,17},{9,25},{17,1},{25,9},{2,18},{10... | collective-permute-start | bytes 4718600 | tf_op jit(solution)/shard_map/ppermute | solution.py:19
  314.5 74.2 %collective-permute-start.16 = (bf16[256,3072]{1,0:T(8,128)(2,1)}, bf16[256,3072]{1,0:T(8,128)(2,1)}, u32[]{:S(2)}, u32[]{:S(2)}) collective-permute-start(bf16[256,3072]{1,0:T(8,128)(2,1)} %get-tuple-element.75), channel_id=1, source_target_pairs={{0,8},{8,0},{16,24},{24,16},{1,9},{9,1},{17,25},{25,17},{2,10},{10... | collective-permute-start | bytes 4718600 | tf_op jit(solution)/shard_map/ppermute | solution.py:19
  333.8 59.7 %collective-permute-start.25 = (bf16[256,3072]{1,0:T(8,128)(2,1)}, bf16[256,3072]{1,0:T(8,128)(2,1)S(1)}, u32[]{:S(2)}, u32[]{:S(2)}) collective-permute-start(bf16[256,3072]{1,0:T(8,128)(2,1)} %get-tuple-element.74), channel_id=1, source_target_pairs={{0,16},{8,24},{16,0},{24,8},{1,17},{9,25},{17,1},{25,9},{2,18},{10... | collective-permute-start | bytes 4718600 | tf_op jit(solution)/shard_map/ppermute | solution.py:19
  355.0 152.6 %collective-permute-start.15 = (bf16[256,3072]{1,0:T(8,128)(2,1)}, bf16[256,3072]{1,0:T(8,128)(2,1)}, u32[]{:S(2)}, u32[]{:S(2)}) collective-permute-start(bf16[256,3072]{1,0:T(8,128)(2,1)} %slice.153), channel_id=1, source_target_pairs={{0,8},{8,0},{16,24},{24,16},{1,9},{9,1},{17,25},{25,17},{2,10},{10... | collective-permute-start | bytes 4718600 | tf_op jit(solution)/shard_map/ppermute | solution.py:19
  380.3 75.8 %collective-permute-start.42 = (bf16[256,3072]{1,0:T(8,128)(2,1)S(1)}, bf16[256,3072]{1,0:T(8,128)(2,1)}, u32[]{:S(2)}, u32[]{:S(2)}) collective-permute-start(bf16[256,3072]{1,0:T(8,128)(2,1)S(1)} %get-tuple-element.53), channel_id=1, source_target_pairs={{0,8},{8,0},{16,24},{24,16},{1,9},{9,1},{17,25},{25,17},{2,10},{10... | collective-permute-start | bytes 4718600 | tf_op jit(solution)/shard_map/ppermute | solution.py:19
  380.6 109.5 %collective-permute-start.44 = (bf16[256,3072]{1,0:T(8,128)(2,1)S(1)}, bf16[256,3072]{1,0:T(8,128)(2,1)S(1)}, u32[]{:S(2)}, u32[]{:S(2)}) collective-permute-start(bf16[256,3072]{1,0:T(8,128)(2,1)S(1)} %get-tuple-element.53), channel_id=1, source_target_pairs={{0,16},{8,24},{16,0},{24,8},{1,17},{9,25},{17,1},{25,9},{2,18},{10... | collective-permute-start | bytes 4718600 | tf_op jit(solution)/shard_map/ppermute | solution.py:19
  388.7 99.7 %collective-permute-start.43 = (bf16[256,3072]{1,0:T(8,128)(2,1)S(1)}, bf16[256,3072]{1,0:T(8,128)(2,1)S(1)}, u32[]{:S(2)}, u32[]{:S(2)}) collective-permute-start(bf16[256,3072]{1,0:T(8,128)(2,1)S(1)} %get-tuple-element.51), channel_id=1, source_target_pairs={{0,8},{8,0},{16,24},{24,16},{1,9},{9,1},{17,25},{25,17},{2,10},{10... | collective-permute-start | bytes 4718600 | tf_op jit(solution)/shard_map/ppermute | solution.py:19
  393.5 114.4 %collective-permute-start.24 = (bf16[256,3072]{1,0:T(8,128)(2,1)S(1)}, bf16[256,3072]{1,0:T(8,128)(2,1)S(1)}, u32[]{:S(2)}, u32[]{:S(2)}) collective-permute-start(bf16[256,3072]{1,0:T(8,128)(2,1)S(1)} %slice.152), channel_id=1, source_target_pairs={{0,16},{8,24},{16,0},{24,8},{1,17},{9,25},{17,1},{25,9},{2,18},{10... | collective-permute-start | bytes 4718600 | tf_op jit(solution)/shard_map/ppermute | solution.py:19
  504.7 55.0 %collective-permute-start.46 = (bf16[256,3072]{1,0:T(8,128)(2,1)}, bf16[256,3072]{1,0:T(8,128)(2,1)}, u32[]{:S(2)}, u32[]{:S(2)}) collective-permute-start(bf16[256,3072]{1,0:T(8,128)(2,1)} %collective-permute-done.42), channel_id=1, source_target_pairs={{0,16},{8,24},{16,0},{24,8},{1,17},{9,25},{17,1},{25,9},{2,18},{10... | collective-permute-start | bytes 4718600 | tf_op jit(solution)/shard_map/ppermute | solution.py:19
  507.6 56.5 %collective-permute-start.47 = (bf16[256,3072]{1,0:T(8,128)(2,1)}, bf16[256,3072]{1,0:T(8,128)(2,1)}, u32[]{:S(2)}, u32[]{:S(2)}) collective-permute-start(bf16[256,3072]{1,0:T(8,128)(2,1)} %collective-permute-done.45), channel_id=1, source_target_pairs={{0,8},{8,0},{16,24},{24,16},{1,9},{9,1},{17,25},{25,17},{2,10},{10... | collective-permute-start | bytes 4718600 | tf_op jit(solution)/shard_map/ppermute | solution.py:19
  551.2 75.4 %collective-permute-start.36 = (bf16[256,3072]{1,0:T(8,128)(2,1)}, bf16[256,3072]{1,0:T(8,128)(2,1)}, u32[]{:S(2)}, u32[]{:S(2)}) collective-permute-start(bf16[256,3072]{1,0:T(8,128)(2,1)} %get-tuple-element.59), channel_id=1, source_target_pairs={{0,8},{8,0},{16,24},{24,16},{1,9},{9,1},{17,25},{25,17},{2,10},{10... | collective-permute-start | bytes 4718600 | tf_op jit(solution)/shard_map/ppermute | solution.py:19
  552.9 79.5 %collective-permute-start.38 = (bf16[256,3072]{1,0:T(8,128)(2,1)}, bf16[256,3072]{1,0:T(8,128)(2,1)}, u32[]{:S(2)}, u32[]{:S(2)}) collective-permute-start(bf16[256,3072]{1,0:T(8,128)(2,1)} %get-tuple-element.59), channel_id=1, source_target_pairs={{0,16},{8,24},{16,0},{24,8},{1,17},{9,25},{17,1},{25,9},{2,18},{10... | collective-permute-start | bytes 4718600 | tf_op jit(solution)/shard_map/ppermute | solution.py:19
  555.9 75.2 %collective-permute-start.37 = (bf16[256,3072]{1,0:T(8,128)(2,1)S(1)}, bf16[256,3072]{1,0:T(8,128)(2,1)S(1)}, u32[]{:S(2)}, u32[]{:S(2)}) collective-permute-start(bf16[256,3072]{1,0:T(8,128)(2,1)S(1)} %get-tuple-element.57), channel_id=1, source_target_pairs={{0,8},{8,0},{16,24},{24,16},{1,9},{9,1},{17,25},{25,17},{2,10},{10... | collective-permute-start | bytes 4718600 | tf_op jit(solution)/shard_map/ppermute | solution.py:19
  559.7 65.3 %collective-permute-start.39 = (bf16[256,3072]{1,0:T(8,128)(2,1)S(1)}, bf16[256,3072]{1,0:T(8,128)(2,1)S(1)}, u32[]{:S(2)}, u32[]{:S(2)}) collective-permute-start(bf16[256,3072]{1,0:T(8,128)(2,1)S(1)} %get-tuple-element.57), channel_id=1, source_target_pairs={{0,16},{8,24},{16,0},{24,8},{1,17},{9,25},{17,1},{25,9},{2,18},{10... | collective-permute-start | bytes 4718600 | tf_op jit(solution)/shard_map/ppermute | solution.py:19
  (42 other events, 879.6 us)
